TPU v7x, 32 devices: a whole 2x2x4 slice. The times are simulated.
32 devices in a mesh: ra: 4 (over x, core), rb: 8 (over z, y).
Axes of the slice: x: 2, y: 2, z: 4, core: 2. Of those that a mesh axis runs over, the one named last changes fastest.
Arguments:
- amplitude: bfloat16 [2, 512, 512, 256], P(None, 'ra', 'rb'), may hold values from -6 to 6
- coupling: bfloat16 [6, 256, 256], replicated, may hold values from -0.5 to 0.5
- pattern: int32 [6, 4, 4], replicated, may hold values 0 or 1
- radial: float32 [6, 512, 512], P(None, 'ra', 'rb'), may hold values from -2.4 to 2.4
- first_prop: bfloat16 [2, 512, 512], replicated, may hold values from -0.1875 to 0.1875
- second_prop: bfloat16 [2, 512, 512], replicated, may hold values from -0.1875 to 0.1875
Outputs:
- evolved: bfloat16 [2, 512, 512, 256], P(None, 'ra', 'rb')
All inputs are finite; a program needn't handle non-finite values.
Results may differ from a plain program's by a relative error of at most 0.0095.
Values may be sent and summed in bfloat16 or wider, within the bound.
A program may use at most 128 MiB of HBM per device.

v0:
```python
import functools

import jax
import jax.numpy as jnp
from jax import lax
from jax.experimental import pallas as pl
from jax.experimental.pallas import tpu as pltpu
from jax.sharding import PartitionSpec as P

KTERMS = 6
STEPS = 2
LANES = 128
TILE = 16
HALF = 8
MESH = pl.DeviceIdType.MESH


def complex_rows(matrix, piece):
    form = "ac,cqw->aqw"
    real_part = jnp.einsum(
        form, matrix[0], piece[0], preferred_element_type=jnp.float32
    ) - jnp.einsum(form, matrix[1], piece[1], preferred_element_type=jnp.float32)
    imag_part = jnp.einsum(
        form, matrix[0], piece[1], preferred_element_type=jnp.float32
    ) + jnp.einsum(form, matrix[1], piece[0], preferred_element_type=jnp.float32)
    return jnp.stack([real_part, imag_part]).astype(jnp.bfloat16)


def masked_weights(coupling, pattern):
    channels = coupling.shape[1]
    count = pattern.shape[1]
    block_size = channels // count
    spread = jnp.broadcast_to(
        pattern[:, :, None, :, None], (KTERMS, count, block_size, count, block_size)
    )
    return coupling * spread.reshape(KTERMS, channels, channels).astype(jnp.bfloat16)


def plain(amplitude, coupling, pattern, radial, first_prop, second_prop):
    first_rows, second_rows, channels = (amplitude.shape[1], amplitude.shape[2], amplitude.shape[3])
    cells = first_rows * second_rows
    groups_a = lax.axis_size("ra")
    groups_b = lax.axis_size("rb")
    width_a = channels // groups_a
    width_b = channels // groups_b
    weights = masked_weights(coupling, pattern)
    radial_cells = radial.reshape(KTERMS, cells).T
    for sweep in range(STEPS):
        flat = amplitude.reshape(2 * cells, channels)
        applied = jnp.einsum("mj,kij->mki", flat, weights, preferred_element_type=jnp.float32)
        applied = applied.reshape(2, cells, KTERMS, channels)
        coupled = jnp.sum(applied * radial_cells[None, :, :, None], axis=2)
        wide = amplitude.reshape(2, cells, channels).astype(jnp.float32)
        kicked = jnp.stack([wide[0] + coupled[1], wide[1] - coupled[0]]).astype(jnp.bfloat16)
        grouped = kicked.reshape(2, first_rows, second_rows, groups_a, width_a)
        grouped = grouped.transpose(0, 1, 3, 2, 4).reshape(
            2, first_rows, groups_a, second_rows * width_a
        )
        half = complex_rows(
            first_prop, lax.all_to_all(grouped, "ra", split_axis=2, concat_axis=1, tiled=True)
        )
        restored = lax.all_to_all(half, "ra", split_axis=1, concat_axis=2, tiled=True)
        restored = restored.reshape(2, first_rows, groups_a, second_rows, width_a)
        restored = restored.transpose(0, 1, 3, 2, 4).reshape(
            2, first_rows, second_rows, groups_b, width_b
        )
        regrouped = restored.transpose(0, 2, 3, 1, 4).reshape(
            2, second_rows, groups_b, first_rows * width_b
        )
        moved = complex_rows(
            second_prop, lax.all_to_all(regrouped, "rb", split_axis=2, concat_axis=1, tiled=True)
        )
        settled = lax.all_to_all(moved, "rb", split_axis=1, concat_axis=2, tiled=True)
        settled = settled.reshape(2, second_rows, groups_b, first_rows, width_b)
        amplitude = settled.transpose(0, 3, 1, 2, 4).reshape(2, first_rows, second_rows, channels)
    return amplitude


def flip(value, mask, bits):
    out = 0
    for n in range(bits):
        weight = 1 << n
        out = out + lax.rem(lax.div(value, weight) + lax.div(mask, weight), 2) * weight
    return out


def fused_kernel(ra, rb, amp_ref, weights_ref, radial_ref, first_ref, second_ref, out_ref,
                 lower, upper, left, right, turn, stage, first_mat, second_mat, near, far,
                 load_sem, store_sem, send_sem, recv_near, recv_far, recv_back, recv_home, rad_send, rad_recv):
    at_a, at_b = lax.axis_index("ra"), lax.axis_index("rb")
    bits_a, bits_b = ra.bit_length() - 1, rb.bit_length() - 1
    chunks = left.shape[1]
    pairs = left.shape[2]
    groups = left.shape[3]
    own = groups // (2 * ra)
    per = pairs * 2
    depth = first_ref.shape[1]
    halfway = lower.shape[1] // 2
    channels = lower.shape[4]
    a_tiles = lower.shape[2]
    devices = ra * rb
    route = [("b", n) for n in reversed(range(bits_b))]
    route = [("b", bits_b - 1), ("a", bits_a - 1)] + [("b", n) for n in range(bits_b - 1)] + [("a", n) for n in range(bits_a - 1)]

    def partner(d):
        mask_a, mask_b = 0, 0
        for n, (axis, bit) in enumerate(route):
            one = lax.rem(lax.div(d, 1 << n), 2) * (1 << bit)
            if axis == "a":
                mask_a = mask_a + one
            else:
                mask_b = mask_b + one
        return flip(at_a, mask_a, bits_a), flip(at_b, mask_b, bits_b)

    barrier = pltpu.get_barrier_semaphore()

    def greet(d, carry):
        to_a, to_b = partner(d)
        pl.semaphore_signal(barrier, inc=1, device_id=(to_a, to_b), device_id_type=MESH)
        return carry

    lax.fori_loop(1, devices, greet, 0)

    def load(q):
        slot = lax.rem(q, 2)
        return pltpu.make_async_copy(amp_ref.at[:, :, pl.ds(q * TILE, TILE)], stage.at[slot], load_sem.at[slot])

    def store(q):
        slot = lax.rem(q, 2)
        return pltpu.make_async_copy(stage.at[slot], out_ref.at[:, :, pl.ds(q * TILE, TILE)], store_sem.at[slot])

    load(jnp.int32(0)).start()
    load(jnp.int32(1)).start()

    for source, target in ((first_ref, first_mat), (second_ref, second_mat)):
        target[:depth, :depth] = source[0]
        target[depth:, depth:] = source[0]
        target[:depth, depth:] = -source[1]
        target[depth:, :depth] = source[1]

    b_rows = amp_ref.shape[2]

    def lay(g, carry):
        block = radial_ref[pl.ds(g * HALF, HALF)].reshape(HALF * HALF, LANES)
        near[g] = jnp.transpose(block)[:b_rows]
        return carry

    lax.fori_loop(0, radial_ref.shape[0] // HALF, lay, 0)

    pl.semaphore_wait(barrier, devices - 1)

    def rad_copy(n):
        to = flip(at_b, n, bits_b)
        return pltpu.make_async_remote_copy(
            src_ref=radial_ref.at[pl.ds(to * TILE, TILE)], dst_ref=far.at[at_b],
            send_sem=rad_send, recv_sem=rad_recv, device_id=(at_a, to), device_id_type=MESH,
        )

    pltpu.make_async_copy(radial_ref.at[pl.ds(at_b * TILE, TILE)], far.at[at_b], rad_recv).start()

    def rad_start(n, carry):
        rad_copy(n).start()
        return carry

    lax.fori_loop(1, rb, rad_start, 0)

    def order_of(b):
        i, r = b // per, b % per
        return i * per + (r % 2) * pairs + r // 2

    places = sorted(range(TILE), key=order_of)

    def kick(planes, factor_of, count):
        both = jnp.concatenate(planes, axis=0)
        total = [None, None]
        for k in range(KTERMS):
            applied = jnp.dot(both, weights_ref[k], preferred_element_type=jnp.float32)
            factor = factor_of(k)
            for p in range(2):
                term = applied[p * count:(p + 1) * count] * factor
                total[p] = term if k == 0 else total[p] + term
        return planes[0].astype(jnp.float32) + total[1], planes[1].astype(jnp.float32) - total[0]

    def kick_chunk(q):
        slot = lax.rem(q, 2)
        load(q).wait()

        def group(g, carry):
            count = TILE * TILE
            planes = [stage[slot, p, pl.ds(g * TILE, TILE)].reshape(count, channels) for p in range(2)]
            laid = [near[g * 2 + n, pl.ds(pl.multiple_of(q * TILE, TILE), TILE)] for n in range(2)]

            def factor_of(k):
                return jnp.concatenate([
                    jnp.broadcast_to(laid[n // HALF][:, (n % HALF) * HALF + k:(n % HALF) * HALF + k + 1], (TILE, channels))
                    for n in range(TILE)
                ], axis=0)

            result = kick(planes, factor_of, count)
            for p in range(2):
                turned = jnp.swapaxes(result[p].reshape(TILE, TILE, channels), 0, 1).astype(jnp.bfloat16)
                for row, b in enumerate(places):
                    lower[p, q * TILE + row, g] = turned[b]
            return carry

        lax.fori_loop(0, a_tiles, group, 0)

        @pl.when(q + 2 < chunks)
        def _():
            load(q + 2).start()

    def near_start(q, d):
        for par in range(2):
            to = flip(at_a, d, bits_a)
            source = lower.at[:, pl.ds(q * TILE + to * per + par * pairs, pairs)]
            target = left.at[:, q, :, pl.ds(par * (groups // 2) + at_a * a_tiles, a_tiles)]
            if d == 0:
                pltpu.make_async_copy(source, target, recv_near.at[q]).start()
            else:
                pltpu.make_async_remote_copy(
                    src_ref=source, dst_ref=target, send_sem=send_sem.at[0], recv_sem=recv_near.at[q],
                    device_id=(to, at_b), device_id_type=MESH,
                ).start()

    def home_start(q, d):
        for par in range(2):
            to = flip(at_a, d, bits_a)
            source = right.at[:, q, :, pl.ds(par * (groups // 2) + to * a_tiles, a_tiles)]
            target = upper.at[:, pl.ds(q * TILE + at_a * per + par * pairs, pairs)]
            if d == 0:
                pltpu.make_async_copy(source, target, recv_home.at[q]).start()
            else:
                pltpu.make_async_remote_copy(
                    src_ref=source, dst_ref=target, send_sem=send_sem.at[3], recv_sem=recv_home.at[q],
                    device_id=(to, at_b), device_id_type=MESH,
                ).start()

    near_order = list(range(ra // 2, ra)) + list(range(1, ra // 2)) + [0]

    def far_start(q, h):
        def place(i, j):
            return (i * rb + j) * 2 + h

        row = h * halfway + at_b * chunks + q

        def one(d, carry):
            to_a, to_b = partner(d)
            pltpu.make_async_remote_copy(
                src_ref=right.at[:, q, :, place(to_a, to_b)], dst_ref=upper.at[:, row, pl.ds(at_a * pairs, pairs)],
                send_sem=send_sem.at[1], recv_sem=recv_far.at[h], device_id=(to_a, to_b), device_id_type=MESH,
            ).start()
            return carry

        lax.fori_loop(1, devices, one, 0)
        pltpu.make_async_copy(
            right.at[:, q, :, place(at_a, at_b)], upper.at[:, row, pl.ds(at_a * pairs, pairs)], recv_far.at[h]
        ).start()

    def back_start(q, h):
        place = (at_a * rb + at_b) * 2 + h

        def one(d, carry):
            to_a, to_b = partner(d)
            pltpu.make_async_remote_copy(
                src_ref=lower.at[:, h * halfway + to_b * chunks + q, pl.ds(to_a * pairs, pairs)],
                dst_ref=left.at[:, q, :, place],
                send_sem=send_sem.at[2], recv_sem=recv_back.at[q], device_id=(to_a, to_b), device_id_type=MESH,
            ).start()
            return carry

        lax.fori_loop(1, devices, one, 0)
        pltpu.make_async_copy(
            lower.at[:, h * halfway + at_b * chunks + q, pl.ds(at_a * pairs, pairs)], left.at[:, q, :, place],
            recv_back.at[q],
        ).start()

    def arrived(ref, sem):
        pltpu.make_async_copy(ref, ref, sem).wait()

    def first_chunk(q):
        arrived(left.at[:, q], recv_near.at[q])

        def pair(bp, carry):
            made = []
            for par in range(2):
                span = pl.ds(par * (groups // 2), groups // 2)
                both = jnp.concatenate([left[p, q, bp, span].reshape(depth, channels) for p in range(2)], axis=0)
                made.append(jnp.dot(first_mat[...], both, preferred_element_type=jnp.float32))
            for p in range(2):
                parts = [m[p * depth:(p + 1) * depth].reshape(groups, HALF, channels) for m in made]
                right[p, q, bp] = jnp.concatenate(parts, axis=1).astype(jnp.bfloat16)
            return carry

        lax.fori_loop(0, pairs, pair, 0)

    def last_chunk(q):
        arrived(left.at[:, q], recv_back.at[q])

        def pair(bp, carry):
            wide = [left[p, q, bp].astype(jnp.float32) for p in range(2)]
            for par in range(2):
                both = jnp.concatenate([
                    w[:, par * HALF:(par + 1) * HALF].reshape(depth, channels).astype(jnp.bfloat16) for w in wide
                ], axis=0)
                made = jnp.dot(first_mat[...], both, preferred_element_type=jnp.float32)
                for p in range(2):
                    right[p, q, bp, pl.ds(par * (groups // 2), groups // 2)] = made[
                        p * depth:(p + 1) * depth].reshape(groups // 2, TILE, channels).astype(jnp.bfloat16)
            return carry

        lax.fori_loop(0, pairs, pair, 0)

    def finish_chunk(q):
        slot = lax.rem(q, 2)
        arrived(upper.at[:, pl.ds(q * TILE, TILE)], recv_home.at[q])

        @pl.when(q >= 2)
        def _():
            store(q - 2).wait()

        def group(g, carry):
            for p in range(2):
                rows = [None] * TILE
                for row, b in enumerate(places):
                    rows[b] = upper[p, q * TILE + row, g].astype(jnp.float32)
                turned = jnp.swapaxes(jnp.stack(rows), 0, 1)
                stage[slot, p, pl.ds(g * TILE, TILE)] = turned.astype(jnp.bfloat16)
            return carry

        lax.fori_loop(0, a_tiles, group, 0)
        store(q).start()

    def opening(t, carry):
        @pl.when(t < chunks)
        def _():
            kick_chunk(t)
            for d in near_order:
                near_start(t, d)

        @pl.when(t >= 2)
        def _():
            q = t - 2
            first_chunk(q)
            far_start(q, 0)

            @pl.when(q < chunks // 2)
            def _():
                far_start(q, 1)

            @pl.when(q == chunks - 1)
            def _():
                def rest(n, carry):
                    far_start(n, 1)
                    return carry

                lax.fori_loop(chunks // 2, chunks, rest, 0)

        return carry

    lax.fori_loop(0, chunks + 2, opening, 0)

    arrived(lower.at[:, 0:lower.shape[1] * (ra - 1) // ra], send_sem.at[0])
    arrived(far, rad_recv)

    width = LANES * 1
    sheets = channels // width
    block = a_tiles * TILE

    def middle(h, carry):
        arrived(upper.at[:, pl.ds(h * halfway, halfway)], recv_far.at[h])

        def spread(m, carry):
            for p in range(2):
                wide = upper[p, h * halfway + m].astype(jnp.float32).reshape(block, channels)
                for s in range(sheets):
                    turn[p, s, pl.ds(pl.multiple_of(m * block, block), block)] = wide[:, s * width:(s + 1) * width]
            return carry

        lax.fori_loop(0, halfway, spread, 0)

        def line(a, carry):
            size = second_ref.shape[1]
            at = pl.ds(a, size, stride=HALF)
            both = jnp.concatenate([
                jnp.concatenate([turn[p, s, at] for s in range(sheets)], axis=1).astype(jnp.bfloat16) for p in range(2)
            ], axis=0)
            made = jnp.dot(second_mat[...], both, preferred_element_type=jnp.float32).astype(jnp.bfloat16)
            laid = jnp.transpose(far[:, h * HALF + a].reshape(rb * HALF, LANES))[:b_rows]

            def factor_of(k):
                return jnp.concatenate([
                    jnp.broadcast_to(laid[:, n * HALF + k:n * HALF + k + 1], (b_rows, channels)) for n in range(rb)
                ], axis=0)

            kicked = kick([made[:size], made[size:]], factor_of, size)
            both = jnp.concatenate([x.astype(jnp.bfloat16) for x in kicked], axis=0)
            made = jnp.dot(second_mat[...], both, preferred_element_type=jnp.float32)
            for p in range(2):
                for s in range(sheets):
                    turn[p, s, at] = made[p * size:(p + 1) * size, s * width:(s + 1) * width]
            return carry

        lax.fori_loop(0, HALF, line, 0)

        def gather(m, carry):
            for p in range(2):
                wide = jnp.concatenate([
                    turn[p, s, pl.ds(pl.multiple_of(m * block, block), block)] for s in range(sheets)
                ], axis=1)
                lower[p, h * halfway + m] = wide.astype(jnp.bfloat16).reshape(a_tiles, TILE, channels)
            return carry

        lax.fori_loop(0, halfway, gather, 0)

        @pl.when(h == 0)
        def _():
            def early(q, carry):
                back_start(q, 0)
                return carry

            lax.fori_loop(0, chunks // 2, early, 0)

        @pl.when(h == 1)
        def _():
            def late(q, carry):
                @pl.when(q >= chunks // 2)
                def _():
                    back_start(q, 0)

                back_start(q, 1)
                return carry

            lax.fori_loop(0, chunks, late, 0)

        return carry

    lax.fori_loop(0, 2, middle, 0)

    arrived(right.at[:, :, :, 0:groups * (devices - 1) // devices], send_sem.at[1])

    def closing(t, carry):
        @pl.when(t < chunks)
        def _():
            last_chunk(t)
            for d in near_order:
                home_start(t, d)

        @pl.when(t >= 1)
        def _():
            finish_chunk(t - 1)

        return carry

    lax.fori_loop(0, chunks + 1, closing, 0)

    store(jnp.int32(chunks - 2)).wait()
    store(jnp.int32(chunks - 1)).wait()
    arrived(lower.at[:, 0:lower.shape[1] * (devices - 1) // devices], send_sem.at[2])
    arrived(right.at[:, :, :, 0:groups * (ra - 1) // ra], send_sem.at[3])
    arrived(far.at[0:rb - 1], rad_send)


def on_device(amplitude, coupling, pattern, radial, first_prop, second_prop):
    a_rows, b_rows, channels = amplitude.shape[1:]
    n_a, n_b = first_prop.shape[1], second_prop.shape[1]
    ra, rb = lax.axis_size("ra"), lax.axis_size("rb")
    devices = ra * rb
    chunks = b_rows // TILE
    fits = (
        channels == 2 * LANES and ra & (ra - 1) == 0 and rb == HALF and ra in (2, 4) and n_a == n_b
        and n_a == TILE * devices and n_b == TILE * devices and a_rows % TILE == 0 and b_rows % TILE == 0
        and chunks % 2 == 0 and chunks == ra and a_rows == TILE * HALF and b_rows <= LANES
    )
    if not fits:
        return plain(amplitude, coupling, pattern, radial, first_prop, second_prop)

    pairs = TILE // ra // 2
    groups = n_a // HALF
    weights = masked_weights(coupling, pattern).transpose(0, 2, 1)
    laid = jnp.pad(radial.transpose(1, 0, 2), ((0, 0), (0, HALF - KTERMS), (0, LANES - b_rows)))
    flat = (2, chunks * TILE, a_rows // TILE, TILE, channels)
    tall = (2, chunks, pairs, groups, TILE, channels)
    whole = pl.BlockSpec(memory_space=pltpu.VMEM)
    kept = pl.BlockSpec(memory_space=pl.ANY)
    dma = pltpu.SemaphoreType.DMA
    return pl.pallas_call(
        functools.partial(fused_kernel, ra, rb),
        in_specs=[kept, whole, whole, whole, whole],
        out_specs=kept,
        out_shape=jax.ShapeDtypeStruct(amplitude.shape, jnp.bfloat16),
        scratch_shapes=[
            pltpu.VMEM(flat, jnp.bfloat16),
            pltpu.VMEM(flat, jnp.bfloat16),
            pltpu.VMEM(tall, jnp.bfloat16),
            pltpu.VMEM(tall, jnp.bfloat16),
            pltpu.VMEM((2, channels // LANES, n_b * HALF, LANES), jnp.float32),
            pltpu.VMEM((2, 2, a_rows, TILE, channels), jnp.bfloat16),
            pltpu.VMEM((2 * n_a, 2 * n_a), jnp.bfloat16),
            pltpu.VMEM((2 * n_b, 2 * n_b), jnp.bfloat16),
            pltpu.VMEM((a_rows // HALF, b_rows, HALF * HALF), jnp.float32),
            pltpu.VMEM((rb, TILE, HALF, LANES), jnp.float32),
            dma((2,)), dma((2,)), dma((4,)), dma((chunks,)), dma((2,)), dma((chunks,)), dma((chunks,)),
            dma(()), dma(()),
        ],
        compiler_params=pltpu.CompilerParams(
            collective_id=0, has_side_effects=True, vmem_limit_bytes=63 * 2**20
        ),
    )(amplitude, weights, laid, first_prop, second_prop)


def solution(mesh):
    return jax.shard_map(
        on_device,
        mesh=mesh,
        in_specs=(P(None, "ra", "rb", None), P(), P(), P(None, "ra", "rb"), P(), P()),
        out_specs=P(None, "ra", "rb", None),
        check_vma=False,
    )
```

profile of v0, /device:TPU:0, one launch (start us, length us, event | category | flops | bytes accessed | tf_op | source)
XLA Modules:
  0.0 456.4 jit_solution(6212326094563350527)
XLA Ops:
  0.0 0.7 convert_element_type.9
  0.7 0.1 copy.7
  0.8 1.2 copy.9
  2.0 0.9 pad.4.radial_ref
  2.9 1.4 copy.8
  4.3 0.5 broadcast_in_dim.2
  4.8 1.0 convert_element_type.10
  5.8 1.0 multiply_bitcast_fusion.weights_ref
  6.7 441.2 %shard_map.64 = bf16[2,128,64,256]{3,2,1,0:T(8,128)(2,1)} custom-call(bf16[2,128,64,256]{3,2,1,0:T(8,128)(2,1)} %amp_ref.1, bf16[6,256,256]{2,1,0:T(8,128)(2,1)} %multiply_bitcast_fusion.weights_ref, f32[128,8,128]{2,1,0:T(8,128)} %pad.4.radial_ref, bf16[2,512,512]{2,1,0:T(8,128)(2,1)} %first_ref.1, bf16[2,512,512]{2,1,0:T(8,128)(2,1)} %second_ref.1), custom_call_target="tpu_custom_call" | custom-call | tf_op jit(solution)/shard_map/pallas_call | solution.py:486
  447.9 8.4 %copy.11 = bf16[2,128,64,256]{3,2,1,0:T(8,128)(2,1)} copy(bf16[2,128,64,256]{3,2,1,0:T(8,128)(2,1)} %shard_map.64) | data formatting | bytes 16777216
where the time goes:
time: 458 us; the launch traced here: 456 us
  Pallas kernels  441 us (96%)
  local copies, waits for them, and re-layouts  13.5 us (3%)
    pallas_call x1, Pallas kernels, on_device(): pl.pallas_call(functools.partial(fused_kernel, ra, rb), in_specs=[kept, w...  441 us
    unnamed x3, local copies, waits for them, and re-layouts  11 us

commit v1 on v0

--- a/solution.py
+++ b/solution.py
@@ -84,23 +84,23 @@
     return out
 
 
-def fused_kernel(ra, rb, amp_ref, weights_ref, radial_ref, first_ref, second_ref, out_ref,
-                 lower, upper, left, right, turn, stage, first_mat, second_mat, near, far,
+def fused_kernel(ra, rb, amp_ref, coupling_ref, pattern_ref, radial_ref, first_ref, second_ref, out_ref,
+                 lower, upper, left, right, turn, stage, first_mat, second_mat, weights_ref, near, far, lines,
                  load_sem, store_sem, send_sem, recv_near, recv_far, recv_back, recv_home, rad_send, rad_recv):
     at_a, at_b = lax.axis_index("ra"), lax.axis_index("rb")
     bits_a, bits_b = ra.bit_length() - 1, rb.bit_length() - 1
     chunks = left.shape[1]
     pairs = left.shape[2]
-    groups = left.shape[3]
-    own = groups // (2 * ra)
+    sixteens = left.shape[4]
+    groups = 2 * sixteens
     per = pairs * 2
     depth = first_ref.shape[1]
     halfway = lower.shape[1] // 2
     channels = lower.shape[4]
     a_tiles = lower.shape[2]
     devices = ra * rb
-    route = [("b", n) for n in reversed(range(bits_b))]
-    route = [("b", bits_b - 1), ("a", bits_a - 1)] + [("b", n) for n in range(bits_b - 1)] + [("a", n) for n in range(bits_a - 1)]
+    route = [("b", bits_b - 1)] + [("b", n) for n in range(bits_b - 1)]
+    route = route + [("a", n) for n in range(bits_a)]
 
     def partner(d):
         mask_a, mask_b = 0, 0
@@ -139,36 +139,44 @@
         target[depth:, :depth] = source[1]
 
     b_rows = amp_ref.shape[2]
+    blocks = pattern_ref.shape[1]
+    size_block = channels // blocks
+    lane = lax.broadcasted_iota(jnp.int32, (size_block, channels), 1)
+    for k in range(KTERMS):
+        masked = []
+        for i in range(blocks):
+            keep = jnp.zeros((size_block, channels), jnp.float32)
+            for j in range(blocks):
+                inside = (lane >= j * size_block) & (lane < (j + 1) * size_block)
+                keep = jnp.where(inside, pattern_ref[k, i, j].astype(jnp.float32), keep)
+            masked.append(coupling_ref[k, i * size_block:(i + 1) * size_block].astype(jnp.float32) * keep)
+        weights_ref[k] = jnp.transpose(jnp.concatenate(masked, axis=0)).astype(jnp.bfloat16)
 
     def lay(g, carry):
-        block = radial_ref[pl.ds(g * HALF, HALF)].reshape(HALF * HALF, LANES)
-        near[g] = jnp.transpose(block)[:b_rows]
+        at = pl.ds(pl.multiple_of(g * HALF, HALF), HALF)
+        near[g] = jnp.transpose(radial_ref[:, at].reshape(KTERMS * HALF, b_rows))
         return carry
 
-    lax.fori_loop(0, radial_ref.shape[0] // HALF, lay, 0)
+    lax.fori_loop(0, radial_ref.shape[1] // HALF, lay, 0)
 
     pl.semaphore_wait(barrier, devices - 1)
 
     def rad_copy(n):
         to = flip(at_b, n, bits_b)
         return pltpu.make_async_remote_copy(
-            src_ref=radial_ref.at[pl.ds(to * TILE, TILE)], dst_ref=far.at[at_b],
+            src_ref=radial_ref.at[:, pl.ds(pl.multiple_of(to * TILE, TILE), TILE)], dst_ref=far.at[at_b],
             send_sem=rad_send, recv_sem=rad_recv, device_id=(at_a, to), device_id_type=MESH,
         )
 
-    pltpu.make_async_copy(radial_ref.at[pl.ds(at_b * TILE, TILE)], far.at[at_b], rad_recv).start()
+    pltpu.make_async_copy(
+        radial_ref.at[:, pl.ds(pl.multiple_of(at_b * TILE, TILE), TILE)], far.at[at_b], rad_recv
+    ).start()
 
     def rad_start(n, carry):
         rad_copy(n).start()
         return carry
 
     lax.fori_loop(1, rb, rad_start, 0)
-
-    def order_of(b):
-        i, r = b // per, b % per
-        return i * per + (r % 2) * pairs + r // 2
-
-    places = sorted(range(TILE), key=order_of)
 
     def kick(planes, factor_of, count):
         both = jnp.concatenate(planes, axis=0)
@@ -192,15 +200,14 @@
 
             def factor_of(k):
                 return jnp.concatenate([
-                    jnp.broadcast_to(laid[n // HALF][:, (n % HALF) * HALF + k:(n % HALF) * HALF + k + 1], (TILE, channels))
+                    jnp.broadcast_to(laid[n // HALF][:, k * HALF + n % HALF:k * HALF + n % HALF + 1], (TILE, channels))
                     for n in range(TILE)
                 ], axis=0)
 
             result = kick(planes, factor_of, count)
             for p in range(2):
                 turned = jnp.swapaxes(result[p].reshape(TILE, TILE, channels), 0, 1).astype(jnp.bfloat16)
-                for row, b in enumerate(places):
-                    lower[p, q * TILE + row, g] = turned[b]
+                lower[p, pl.ds(q * TILE, TILE), g] = turned
             return carry
 
         lax.fori_loop(0, a_tiles, group, 0)
@@ -209,106 +216,114 @@
         def _():
             load(q + 2).start()
 
-    def near_start(q, d):
-        for par in range(2):
-            to = flip(at_a, d, bits_a)
-            source = lower.at[:, pl.ds(q * TILE + to * per + par * pairs, pairs)]
-            target = left.at[:, q, :, pl.ds(par * (groups // 2) + at_a * a_tiles, a_tiles)]
-            if d == 0:
-                pltpu.make_async_copy(source, target, recv_near.at[q]).start()
-            else:
-                pltpu.make_async_remote_copy(
-                    src_ref=source, dst_ref=target, send_sem=send_sem.at[0], recv_sem=recv_near.at[q],
-                    device_id=(to, at_b), device_id_type=MESH,
-                ).start()
-
-    def home_start(q, d):
-        for par in range(2):
-            to = flip(at_a, d, bits_a)
-            source = right.at[:, q, :, pl.ds(par * (groups // 2) + to * a_tiles, a_tiles)]
-            target = upper.at[:, pl.ds(q * TILE + at_a * per + par * pairs, pairs)]
-            if d == 0:
-                pltpu.make_async_copy(source, target, recv_home.at[q]).start()
-            else:
-                pltpu.make_async_remote_copy(
-                    src_ref=source, dst_ref=target, send_sem=send_sem.at[3], recv_sem=recv_home.at[q],
-                    device_id=(to, at_b), device_id_type=MESH,
-                ).start()
+    def near_start(q, bp, d):
+        to = flip(at_a, d, bits_a)
+        source = lower.at[:, pl.ds(q * TILE + to * per + bp * 2, 2)]
+        target = left.at[:, q, bp, :, pl.ds(at_a * a_tiles, a_tiles)]
+        sem = recv_near.at[q * pairs + bp]
+        if d == 0:
+            pltpu.make_async_copy(source, target, sem).start()
+        else:
+            pltpu.make_async_remote_copy(
+                src_ref=source, dst_ref=target, send_sem=send_sem.at[0], recv_sem=sem,
+                device_id=(to, at_b), device_id_type=MESH,
+            ).start()
+
+    def home_start(q, bp, d):
+        to = flip(at_a, d, bits_a)
+        source = right.at[:, q, bp, :, pl.ds(to * a_tiles, a_tiles)]
+        target = upper.at[:, pl.ds(q * TILE + at_a * per + bp * 2, 2)]
+        if d == 0:
+            pltpu.make_async_copy(source, target, recv_home.at[q]).start()
+        else:
+            pltpu.make_async_remote_copy(
+                src_ref=source, dst_ref=target, send_sem=send_sem.at[3], recv_sem=recv_home.at[q],
+                device_id=(to, at_b), device_id_type=MESH,
+            ).start()
 
     near_order = list(range(ra // 2, ra)) + list(range(1, ra // 2)) + [0]
-
-    def far_start(q, h):
-        def place(i, j):
-            return (i * rb + j) * 2 + h
-
+    side = devices // 2
+
+    def place(i, j, h):
+        index = (i * rb + j) * 2 + h
+        return lax.div(index, sixteens), lax.rem(index, sixteens)
+
+    def far_start(c, h, crossing):
+        q, bp = lax.div(c, pairs), lax.rem(c, pairs)
         row = h * halfway + at_b * chunks + q
+        target = upper.at[:, row, at_a * pairs + bp]
+
+        def one(d, carry):
+            to_a, to_b = partner(d)
+            high, low = place(to_a, to_b, h)
+            pltpu.make_async_remote_copy(
+                src_ref=right.at[:, q, bp, high, low], dst_ref=target,
+                send_sem=send_sem.at[1], recv_sem=recv_far.at[h], device_id=(to_a, to_b), device_id_type=MESH,
+            ).start()
+            return carry
+
+        if crossing:
+            lax.fori_loop(side, devices, one, 0)
+        else:
+            lax.fori_loop(1, side, one, 0)
+            high, low = place(at_a, at_b, h)
+            pltpu.make_async_copy(right.at[:, q, bp, high, low], target, recv_far.at[h]).start()
+
+    def back_start(c, h, crossing):
+        q, bp = lax.div(c, pairs), lax.rem(c, pairs)
+        high, low = place(at_a, at_b, h)
+        target = left.at[:, q, bp, high, low]
 
         def one(d, carry):
             to_a, to_b = partner(d)
             pltpu.make_async_remote_copy(
-                src_ref=right.at[:, q, :, place(to_a, to_b)], dst_ref=upper.at[:, row, pl.ds(at_a * pairs, pairs)],
-                send_sem=send_sem.at[1], recv_sem=recv_far.at[h], device_id=(to_a, to_b), device_id_type=MESH,
+                src_ref=lower.at[:, h * halfway + to_b * chunks + q, to_a * pairs + bp], dst_ref=target,
+                send_sem=send_sem.at[2], recv_sem=recv_back.at[c], device_id=(to_a, to_b), device_id_type=MESH,
             ).start()
             return carry
 
-        lax.fori_loop(1, devices, one, 0)
-        pltpu.make_async_copy(
-            right.at[:, q, :, place(at_a, at_b)], upper.at[:, row, pl.ds(at_a * pairs, pairs)], recv_far.at[h]
-        ).start()
-
-    def back_start(q, h):
-        place = (at_a * rb + at_b) * 2 + h
-
-        def one(d, carry):
-            to_a, to_b = partner(d)
-            pltpu.make_async_remote_copy(
-                src_ref=lower.at[:, h * halfway + to_b * chunks + q, pl.ds(to_a * pairs, pairs)],
-                dst_ref=left.at[:, q, :, place],
-                send_sem=send_sem.at[2], recv_sem=recv_back.at[q], device_id=(to_a, to_b), device_id_type=MESH,
+        if crossing:
+            lax.fori_loop(side, devices, one, 0)
+        else:
+            lax.fori_loop(1, side, one, 0)
+            pltpu.make_async_copy(
+                lower.at[:, h * halfway + at_b * chunks + q, at_a * pairs + bp], target, recv_back.at[c]
             ).start()
-            return carry
-
-        lax.fori_loop(1, devices, one, 0)
-        pltpu.make_async_copy(
-            lower.at[:, h * halfway + at_b * chunks + q, pl.ds(at_a * pairs, pairs)], left.at[:, q, :, place],
-            recv_back.at[q],
-        ).start()
+
+    def every(action):
+        def one(c, carry):
+            action(c)
+            return carry
+
+        lax.fori_loop(0, chunks * pairs, one, 0)
 
     def arrived(ref, sem):
         pltpu.make_async_copy(ref, ref, sem).wait()
 
-    def first_chunk(q):
-        arrived(left.at[:, q], recv_near.at[q])
-
-        def pair(bp, carry):
-            made = []
-            for par in range(2):
-                span = pl.ds(par * (groups // 2), groups // 2)
-                both = jnp.concatenate([left[p, q, bp, span].reshape(depth, channels) for p in range(2)], axis=0)
-                made.append(jnp.dot(first_mat[...], both, preferred_element_type=jnp.float32))
-            for p in range(2):
-                parts = [m[p * depth:(p + 1) * depth].reshape(groups, HALF, channels) for m in made]
-                right[p, q, bp] = jnp.concatenate(parts, axis=1).astype(jnp.bfloat16)
-            return carry
-
-        lax.fori_loop(0, pairs, pair, 0)
-
-    def last_chunk(q):
-        arrived(left.at[:, q], recv_back.at[q])
-
-        def pair(bp, carry):
-            wide = [left[p, q, bp].astype(jnp.float32) for p in range(2)]
-            for par in range(2):
-                both = jnp.concatenate([
-                    w[:, par * HALF:(par + 1) * HALF].reshape(depth, channels).astype(jnp.bfloat16) for w in wide
-                ], axis=0)
-                made = jnp.dot(first_mat[...], both, preferred_element_type=jnp.float32)
-                for p in range(2):
-                    right[p, q, bp, pl.ds(par * (groups // 2), groups // 2)] = made[
-                        p * depth:(p + 1) * depth].reshape(groups // 2, TILE, channels).astype(jnp.bfloat16)
-            return carry
-
-        lax.fori_loop(0, pairs, pair, 0)
+    def first_chunk(c):
+        q, bp = lax.div(c, pairs), lax.rem(c, pairs)
+        arrived(left.at[:, q, bp], recv_near.at[c])
+        made = []
+        for par in range(2):
+            both = jnp.concatenate([left[p, q, bp, par].reshape(depth, channels) for p in range(2)], axis=0)
+            made.append(jnp.dot(first_mat[...], both, preferred_element_type=jnp.float32))
+        for p in range(2):
+            parts = [m[p * depth:(p + 1) * depth].reshape(groups, HALF, channels) for m in made]
+            mixed = jnp.concatenate(parts, axis=1).astype(jnp.bfloat16)
+            right[p, q, bp] = mixed.reshape(2, sixteens, TILE, channels)
+
+    def last_chunk(c):
+        q, bp = lax.div(c, pairs), lax.rem(c, pairs)
+        arrived(left.at[:, q, bp], recv_back.at[c])
+        wide = [left[p, q, bp].reshape(groups, TILE, channels).astype(jnp.float32) for p in range(2)]
+        for par in range(2):
+            both = jnp.concatenate([
+                w[:, par * HALF:(par + 1) * HALF].reshape(depth, channels).astype(jnp.bfloat16) for w in wide
+            ], axis=0)
+            made = jnp.dot(first_mat[...], both, preferred_element_type=jnp.float32)
+            for p in range(2):
+                part = made[p * depth:(p + 1) * depth].reshape(sixteens, TILE, channels)
+                right[p, q, bp, par] = part.astype(jnp.bfloat16)
 
     def finish_chunk(q):
         slot = lax.rem(q, 2)
@@ -320,10 +335,7 @@
 
         def group(g, carry):
             for p in range(2):
-                rows = [None] * TILE
-                for row, b in enumerate(places):
-                    rows[b] = upper[p, q * TILE + row, g].astype(jnp.float32)
-                turned = jnp.swapaxes(jnp.stack(rows), 0, 1)
+                turned = jnp.swapaxes(upper[p, pl.ds(q * TILE, TILE), g].astype(jnp.float32), 0, 1)
                 stage[slot, p, pl.ds(g * TILE, TILE)] = turned.astype(jnp.bfloat16)
             return carry
 
@@ -334,30 +346,25 @@
         @pl.when(t < chunks)
         def _():
             kick_chunk(t)
-            for d in near_order:
-                near_start(t, d)
-
-        @pl.when(t >= 2)
+            for bp in range(pairs):
+                for d in near_order:
+                    near_start(t, bp, d)
+
+        @pl.when(t >= 1)
         def _():
-            q = t - 2
-            first_chunk(q)
-            far_start(q, 0)
-
-            @pl.when(q < chunks // 2)
-            def _():
-                far_start(q, 1)
-
-            @pl.when(q == chunks - 1)
-            def _():
-                def rest(n, carry):
-                    far_start(n, 1)
-                    return carry
-
-                lax.fori_loop(chunks // 2, chunks, rest, 0)
+            def one(c, carry):
+                first_chunk(c)
+                far_start(c, 0, False)
+                far_start(c, 1, False)
+                return carry
+
+            lax.fori_loop((t - 1) * pairs, t * pairs, one, 0)
 
         return carry
 
-    lax.fori_loop(0, chunks + 2, opening, 0)
+    lax.fori_loop(0, chunks + 1, opening, 0)
+    every(lambda c: far_start(c, 0, True))
+    every(lambda c: far_start(c, 1, True))
 
     arrived(lower.at[:, 0:lower.shape[1] * (ra - 1) // ra], send_sem.at[0])
     arrived(far, rad_recv)
@@ -368,6 +375,8 @@
 
     def middle(h, carry):
         arrived(upper.at[:, pl.ds(h * halfway, halfway)], recv_far.at[h])
+        pieces = far[:, :, pl.ds(pl.multiple_of(h * HALF, HALF), HALF)].reshape(rb * KTERMS, HALF, b_rows)
+        lines[...] = jnp.swapaxes(pieces, 0, 1)
 
         def spread(m, carry):
             for p in range(2):
@@ -385,11 +394,11 @@
                 jnp.concatenate([turn[p, s, at] for s in range(sheets)], axis=1).astype(jnp.bfloat16) for p in range(2)
             ], axis=0)
             made = jnp.dot(second_mat[...], both, preferred_element_type=jnp.float32).astype(jnp.bfloat16)
-            laid = jnp.transpose(far[:, h * HALF + a].reshape(rb * HALF, LANES))[:b_rows]
+            laid = jnp.transpose(lines[a])
 
             def factor_of(k):
                 return jnp.concatenate([
-                    jnp.broadcast_to(laid[:, n * HALF + k:n * HALF + k + 1], (b_rows, channels)) for n in range(rb)
+                    jnp.broadcast_to(laid[:, n * KTERMS + k:n * KTERMS + k + 1], (b_rows, channels)) for n in range(rb)
                 ], axis=0)
 
             kicked = kick([made[:size], made[size:]], factor_of, size)
@@ -412,38 +421,28 @@
 
         lax.fori_loop(0, halfway, gather, 0)
 
-        @pl.when(h == 0)
-        def _():
-            def early(q, carry):
-                back_start(q, 0)
-                return carry
-
-            lax.fori_loop(0, chunks // 2, early, 0)
-
-        @pl.when(h == 1)
-        def _():
-            def late(q, carry):
-                @pl.when(q >= chunks // 2)
-                def _():
-                    back_start(q, 0)
-
-                back_start(q, 1)
-                return carry
-
-            lax.fori_loop(0, chunks, late, 0)
-
+        every(lambda c: back_start(c, h, True))
         return carry
 
     lax.fori_loop(0, 2, middle, 0)
 
-    arrived(right.at[:, :, :, 0:groups * (devices - 1) // devices], send_sem.at[1])
+    def rest(c):
+        back_start(c, 0, False)
+        back_start(c, 1, False)
+
+    every(rest)
+    arrived(right.at[:, :, :, :, 0:sixteens * (devices - 1) // devices], send_sem.at[1])
 
     def closing(t, carry):
         @pl.when(t < chunks)
         def _():
-            last_chunk(t)
-            for d in near_order:
-                home_start(t, d)
+            def one(c, carry):
+                last_chunk(c)
+                for d in near_order:
+                    home_start(t, lax.rem(c, pairs), d)
+                return carry
+
+            lax.fori_loop(t * pairs, (t + 1) * pairs, one, 0)
 
         @pl.when(t >= 1)
         def _():
@@ -456,7 +455,7 @@
     store(jnp.int32(chunks - 2)).wait()
     store(jnp.int32(chunks - 1)).wait()
     arrived(lower.at[:, 0:lower.shape[1] * (devices - 1) // devices], send_sem.at[2])
-    arrived(right.at[:, :, :, 0:groups * (ra - 1) // ra], send_sem.at[3])
+    arrived(right.at[:, :, :, :, 0:sixteens * (ra - 1) // ra], send_sem.at[3])
     arrived(far.at[0:rb - 1], rad_send)
 
 
@@ -476,16 +475,14 @@
 
     pairs = TILE // ra // 2
     groups = n_a // HALF
-    weights = masked_weights(coupling, pattern).transpose(0, 2, 1)
-    laid = jnp.pad(radial.transpose(1, 0, 2), ((0, 0), (0, HALF - KTERMS), (0, LANES - b_rows)))
     flat = (2, chunks * TILE, a_rows // TILE, TILE, channels)
-    tall = (2, chunks, pairs, groups, TILE, channels)
+    tall = (2, chunks, pairs, 2, groups // 2, TILE, channels)
     whole = pl.BlockSpec(memory_space=pltpu.VMEM)
     kept = pl.BlockSpec(memory_space=pl.ANY)
     dma = pltpu.SemaphoreType.DMA
     return pl.pallas_call(
         functools.partial(fused_kernel, ra, rb),
-        in_specs=[kept, whole, whole, whole, whole],
+        in_specs=[kept, whole, pl.BlockSpec(memory_space=pltpu.SMEM), whole, whole, whole],
         out_specs=kept,
         out_shape=jax.ShapeDtypeStruct(amplitude.shape, jnp.bfloat16),
         scratch_shapes=[
@@ -497,15 +494,17 @@
             pltpu.VMEM((2, 2, a_rows, TILE, channels), jnp.bfloat16),
             pltpu.VMEM((2 * n_a, 2 * n_a), jnp.bfloat16),
             pltpu.VMEM((2 * n_b, 2 * n_b), jnp.bfloat16),
-            pltpu.VMEM((a_rows // HALF, b_rows, HALF * HALF), jnp.float32),
-            pltpu.VMEM((rb, TILE, HALF, LANES), jnp.float32),
-            dma((2,)), dma((2,)), dma((4,)), dma((chunks,)), dma((2,)), dma((chunks,)), dma((chunks,)),
+            pltpu.VMEM((KTERMS, channels, channels), jnp.bfloat16),
+            pltpu.VMEM((a_rows // HALF, b_rows, KTERMS * HALF), jnp.float32),
+            pltpu.VMEM((rb, KTERMS, TILE, b_rows), jnp.float32),
+            pltpu.VMEM((HALF, rb * KTERMS, b_rows), jnp.float32),
+            dma((2,)), dma((2,)), dma((4,)), dma((chunks * pairs,)), dma((2,)), dma((chunks * pairs,)), dma((chunks,)),
             dma(()), dma(()),
         ],
         compiler_params=pltpu.CompilerParams(
             collective_id=0, has_side_effects=True, vmem_limit_bytes=63 * 2**20
         ),
-    )(amplitude, weights, laid, first_prop, second_prop)
+    )(amplitude, coupling, pattern, radial, first_prop, second_prop)
 
 
 def solution(mesh):

time: 458 us -> 468 us (1.022)
  Pallas kernels: 441 us -> 456 us
    pallas_call x1, Pallas kernels: 441 us -> 456 us  [on_device(): pl.pallas_call(functools.partial(fused_kernel, ra, rb), in_specs=[kept, w...]
where the time goes in v1:
time: 468 us; the launch traced here: 467 us
  Pallas kernels  456 us (97%)
  local copies, waits for them, and re-layouts  11.7 us (2%)
    pallas_call x1, Pallas kernels, on_device(): pl.pallas_call(functools.partial(fused_kernel, ra, rb), in_specs=[kept, w...  456 us
    unnamed x3, local copies, waits for them, and re-layouts  11.7 us

profile of v1, /device:TPU:0, one launch (start us, length us, event | category | flops | bytes accessed | tf_op | source)
XLA Modules:
  0.0 467.5 jit_solution(10563096119728758883)
XLA Ops:
  0.0 1.4 copy.7.pattern_ref
  1.4 1.8 copy.8.radial_ref
  3.2 455.8 %shard_map.64 = bf16[2,128,64,256]{3,2,1,0:T(8,128)(2,1)} custom-call(bf16[2,128,64,256]{3,2,1,0:T(8,128)(2,1)} %amp_ref.1, bf16[6,256,256]{2,1,0:T(8,128)(2,1)} %coupling_ref.1, s32[6,4,4]{2,1,0:T(4,128)} %copy.7.pattern_ref, f32[6,128,64]{2,1,0:T(8,128)} %copy.8.radial_ref, bf16[2,512,512]{2,1,0:T(8,128)(2,1)} %first_ref.1, bf16[2,512,512]{2,1,0:T(8,128)(2,1)} %second_ref.1), custom_call_target="tpu_custom_call" | custom-call | tf_op jit(solution)/shard_map/pallas_call | solution.py:483
  459.0 8.4 %copy.10 = bf16[2,128,64,256]{3,2,1,0:T(8,128)(2,1)} copy(bf16[2,128,64,256]{3,2,1,0:T(8,128)(2,1)} %shard_map.64) | data formatting | bytes 16777216

commit v2 on v1

--- a/solution.py
+++ b/solution.py
@@ -76,6 +76,10 @@
     return amplitude
 
 
+BACK_LEAD = 2
+FAR_LEAD = 2
+
+
 def flip(value, mask, bits):
     out = 0
     for n in range(bits):
@@ -84,8 +88,8 @@
     return out
 
 
-def fused_kernel(ra, rb, amp_ref, coupling_ref, pattern_ref, radial_ref, first_ref, second_ref, out_ref,
-                 lower, upper, left, right, turn, stage, first_mat, second_mat, weights_ref, near, far, lines,
+def fused_kernel(ra, rb, amp_ref, coupling_ref, pattern_ref, turned_ref, first_ref, second_ref, out_ref,
+                 lower, upper, left, right, turn, stage, first_mat, second_mat, weights_ref, radial_ref, near, far, lines,
                  load_sem, store_sem, send_sem, recv_near, recv_far, recv_back, recv_home, rad_send, rad_recv):
     at_a, at_b = lax.axis_index("ra"), lax.axis_index("rb")
     bits_a, bits_b = ra.bit_length() - 1, rb.bit_length() - 1
@@ -126,20 +130,14 @@
         return pltpu.make_async_copy(amp_ref.at[:, :, pl.ds(q * TILE, TILE)], stage.at[slot], load_sem.at[slot])
 
     def store(q):
-        slot = lax.rem(q, 2)
-        return pltpu.make_async_copy(stage.at[slot], out_ref.at[:, :, pl.ds(q * TILE, TILE)], store_sem.at[slot])
+        tile = pl.ds(q * TILE, TILE)
+        return pltpu.make_async_copy(upper.at[:, tile], out_ref.at[:, tile], store_sem)
 
     load(jnp.int32(0)).start()
     load(jnp.int32(1)).start()
 
-    for source, target in ((first_ref, first_mat), (second_ref, second_mat)):
-        target[:depth, :depth] = source[0]
-        target[depth:, depth:] = source[0]
-        target[:depth, depth:] = -source[1]
-        target[depth:, :depth] = source[1]
-
     b_rows = amp_ref.shape[2]
-    blocks = pattern_ref.shape[1]
+    blocks = pattern_ref.shape[0]
     size_block = channels // blocks
     lane = lax.broadcasted_iota(jnp.int32, (size_block, channels), 1)
     for k in range(KTERMS):
@@ -148,9 +146,12 @@
             keep = jnp.zeros((size_block, channels), jnp.float32)
             for j in range(blocks):
                 inside = (lane >= j * size_block) & (lane < (j + 1) * size_block)
-                keep = jnp.where(inside, pattern_ref[k, i, j].astype(jnp.float32), keep)
+                keep = jnp.where(inside, pattern_ref[i, j, k].astype(jnp.float32), keep)
             masked.append(coupling_ref[k, i * size_block:(i + 1) * size_block].astype(jnp.float32) * keep)
         weights_ref[k] = jnp.transpose(jnp.concatenate(masked, axis=0)).astype(jnp.bfloat16)
+
+    for k in range(KTERMS):
+        radial_ref[k] = jnp.transpose(turned_ref[k])
 
     def lay(g, carry):
         at = pl.ds(pl.multiple_of(g * HALF, HALF), HALF)
@@ -158,25 +159,6 @@
         return carry
 
     lax.fori_loop(0, radial_ref.shape[1] // HALF, lay, 0)
-
-    pl.semaphore_wait(barrier, devices - 1)
-
-    def rad_copy(n):
-        to = flip(at_b, n, bits_b)
-        return pltpu.make_async_remote_copy(
-            src_ref=radial_ref.at[:, pl.ds(pl.multiple_of(to * TILE, TILE), TILE)], dst_ref=far.at[at_b],
-            send_sem=rad_send, recv_sem=rad_recv, device_id=(at_a, to), device_id_type=MESH,
-        )
-
-    pltpu.make_async_copy(
-        radial_ref.at[:, pl.ds(pl.multiple_of(at_b * TILE, TILE), TILE)], far.at[at_b], rad_recv
-    ).start()
-
-    def rad_start(n, carry):
-        rad_copy(n).start()
-        return carry
-
-    lax.fori_loop(1, rb, rad_start, 0)
 
     def kick(planes, factor_of, count):
         both = jnp.concatenate(planes, axis=0)
@@ -326,45 +308,63 @@
                 right[p, q, bp, par] = part.astype(jnp.bfloat16)
 
     def finish_chunk(q):
-        slot = lax.rem(q, 2)
         arrived(upper.at[:, pl.ds(q * TILE, TILE)], recv_home.at[q])
-
-        @pl.when(q >= 2)
-        def _():
-            store(q - 2).wait()
-
-        def group(g, carry):
-            for p in range(2):
-                turned = jnp.swapaxes(upper[p, pl.ds(q * TILE, TILE), g].astype(jnp.float32), 0, 1)
-                stage[slot, p, pl.ds(g * TILE, TILE)] = turned.astype(jnp.bfloat16)
-            return carry
-
-        lax.fori_loop(0, a_tiles, group, 0)
         store(q).start()
+
+    def near_all(q):
+        for bp in range(pairs):
+            for d in near_order:
+                near_start(q, bp, d)
+
+    kick_chunk(jnp.int32(0))
+    pl.semaphore_wait(barrier, devices - 1)
+    near_all(jnp.int32(0))
+
+    def rad_copy(n):
+        to = flip(at_b, n, bits_b)
+        return pltpu.make_async_remote_copy(
+            src_ref=radial_ref.at[:, pl.ds(pl.multiple_of(to * TILE, TILE), TILE)], dst_ref=far.at[at_b],
+            send_sem=rad_send, recv_sem=rad_recv, device_id=(at_a, to), device_id_type=MESH,
+        )
+
+    pltpu.make_async_copy(
+        radial_ref.at[:, pl.ds(pl.multiple_of(at_b * TILE, TILE), TILE)], far.at[at_b], rad_recv
+    ).start()
+
+    def rad_start(n, carry):
+        rad_copy(n).start()
+        return carry
+
+    lax.fori_loop(1, rb, rad_start, 0)
+
+    for source, target in ((first_ref, first_mat), (second_ref, second_mat)):
+        target[:depth, :depth] = source[0]
+        target[depth:, depth:] = source[0]
+        target[:depth, depth:] = -source[1]
+        target[depth:, :depth] = source[1]
 
     def opening(t, carry):
         @pl.when(t < chunks)
         def _():
             kick_chunk(t)
-            for bp in range(pairs):
-                for d in near_order:
-                    near_start(t, bp, d)
-
-        @pl.when(t >= 1)
-        def _():
-            def one(c, carry):
-                first_chunk(c)
-                far_start(c, 0, False)
-                far_start(c, 1, False)
-                return carry
-
-            lax.fori_loop((t - 1) * pairs, t * pairs, one, 0)
-
-        return carry
-
-    lax.fori_loop(0, chunks + 1, opening, 0)
-    every(lambda c: far_start(c, 0, True))
-    every(lambda c: far_start(c, 1, True))
+            near_all(t)
+
+        def one(c, carry):
+            first_chunk(c)
+            far_start(c, 0, False)
+            far_start(c, 1, False)
+            return carry
+
+        lax.fori_loop((t - 1) * pairs, t * pairs, one, 0)
+        return carry
+
+    lax.fori_loop(1, chunks + 1, opening, 0)
+    def crossing(c, h):
+        far_start(c, h, True)
+        return h
+
+    lax.fori_loop(0, chunks * pairs, crossing, 0)
+    lax.fori_loop(0, FAR_LEAD, crossing, 1)
 
     arrived(lower.at[:, 0:lower.shape[1] * (ra - 1) // ra], send_sem.at[0])
     arrived(far, rad_recv)
@@ -375,6 +375,11 @@
 
     def middle(h, carry):
         arrived(upper.at[:, pl.ds(h * halfway, halfway)], recv_far.at[h])
+
+        @pl.when(h == 0)
+        def _():
+            lax.fori_loop(FAR_LEAD, chunks * pairs, crossing, 1)
+
         pieces = far[:, :, pl.ds(pl.multiple_of(h * HALF, HALF), HALF)].reshape(rb * KTERMS, HALF, b_rows)
         lines[...] = jnp.swapaxes(pieces, 0, 1)
 
@@ -426,11 +431,12 @@
 
     lax.fori_loop(0, 2, middle, 0)
 
-    def rest(c):
+    def rest(c, carry):
         back_start(c, 0, False)
         back_start(c, 1, False)
-
-    every(rest)
+        return carry
+
+    lax.fori_loop(0, BACK_LEAD, rest, 0)
     arrived(right.at[:, :, :, :, 0:sixteens * (devices - 1) // devices], send_sem.at[1])
 
     def closing(t, carry):
@@ -440,6 +446,11 @@
                 last_chunk(c)
                 for d in near_order:
                     home_start(t, lax.rem(c, pairs), d)
+
+                @pl.when(c + BACK_LEAD < chunks * pairs)
+                def _():
+                    rest(c + BACK_LEAD, 0)
+
                 return carry
 
             lax.fori_loop(t * pairs, (t + 1) * pairs, one, 0)
@@ -452,11 +463,32 @@
 
     lax.fori_loop(0, chunks + 1, closing, 0)
 
-    store(jnp.int32(chunks - 2)).wait()
-    store(jnp.int32(chunks - 1)).wait()
+    pltpu.make_async_copy(upper, out_ref, store_sem).wait()
     arrived(lower.at[:, 0:lower.shape[1] * (devices - 1) // devices], send_sem.at[2])
     arrived(right.at[:, :, :, :, 0:sixteens * (ra - 1) // ra], send_sem.at[3])
     arrived(far.at[0:rb - 1], rad_send)
+
+
+def unfold_kernel(in_ref, out_ref):
+    def group(g, carry):
+        for p in range(2):
+            turned = jnp.swapaxes(in_ref[p, :, g].astype(jnp.float32), 0, 1)
+            out_ref[p, pl.ds(g * TILE, TILE)] = turned.astype(jnp.bfloat16)
+        return carry
+
+    lax.fori_loop(0, in_ref.shape[2], group, 0)
+
+
+def unfold(folded, shape):
+    tiles = shape[1] // TILE
+    part = tiles // 2
+    return pl.pallas_call(
+        unfold_kernel,
+        grid=(shape[2] // TILE, tiles // part),
+        in_specs=[pl.BlockSpec((2, TILE, part, TILE, shape[3]), lambda q, g: (0, q, g, 0, 0))],
+        out_specs=pl.BlockSpec((2, part * TILE, TILE, shape[3]), lambda q, g: (0, g, q, 0)),
+        out_shape=jax.ShapeDtypeStruct(shape, jnp.bfloat16),
+    )(folded)
 
 
 def on_device(amplitude, coupling, pattern, radial, first_prop, second_prop):
@@ -480,11 +512,11 @@
     whole = pl.BlockSpec(memory_space=pltpu.VMEM)
     kept = pl.BlockSpec(memory_space=pl.ANY)
     dma = pltpu.SemaphoreType.DMA
-    return pl.pallas_call(
+    folded = pl.pallas_call(
         functools.partial(fused_kernel, ra, rb),
         in_specs=[kept, whole, pl.BlockSpec(memory_space=pltpu.SMEM), whole, whole, whole],
         out_specs=kept,
-        out_shape=jax.ShapeDtypeStruct(amplitude.shape, jnp.bfloat16),
+        out_shape=jax.ShapeDtypeStruct(flat, jnp.bfloat16),
         scratch_shapes=[
             pltpu.VMEM(flat, jnp.bfloat16),
             pltpu.VMEM(flat, jnp.bfloat16),
@@ -495,16 +527,18 @@
             pltpu.VMEM((2 * n_a, 2 * n_a), jnp.bfloat16),
             pltpu.VMEM((2 * n_b, 2 * n_b), jnp.bfloat16),
             pltpu.VMEM((KTERMS, channels, channels), jnp.bfloat16),
+            pltpu.VMEM((KTERMS, a_rows, b_rows), jnp.float32),
             pltpu.VMEM((a_rows // HALF, b_rows, KTERMS * HALF), jnp.float32),
             pltpu.VMEM((rb, KTERMS, TILE, b_rows), jnp.float32),
             pltpu.VMEM((HALF, rb * KTERMS, b_rows), jnp.float32),
-            dma((2,)), dma((2,)), dma((4,)), dma((chunks * pairs,)), dma((2,)), dma((chunks * pairs,)), dma((chunks,)),
+            dma((2,)), dma(()), dma((4,)), dma((chunks * pairs,)), dma((2,)), dma((chunks * pairs,)), dma((chunks,)),
             dma(()), dma(()),
         ],
         compiler_params=pltpu.CompilerParams(
             collective_id=0, has_side_effects=True, vmem_limit_bytes=63 * 2**20
         ),
-    )(amplitude, coupling, pattern, radial, first_prop, second_prop)
+    )(amplitude, coupling, pattern.transpose(1, 2, 0), radial.transpose(0, 2, 1), first_prop, second_prop)
+    return unfold(folded, amplitude.shape)
 
 
 def solution(mesh):

time: 468 us -> 421 us (0.90)
  Pallas kernels: 456 us -> 419 us
  local copies, waits for them, and re-layouts: 11.7 us -> 0 us
    pallas_call x1, Pallas kernels: 456 us -> 409 us  [on_device(): pl.pallas_call(functools.partial(fused_kernel, ra, rb), in_specs=[kept, w...]
    unnamed x3 -> x0, local copies, waits for them, and re-layouts: 11.7 us -> none
    pallas_call x0 -> x1, Pallas kernels: none -> 10.8 us  [unfold(): pl.pallas_call(unfold_kernel, grid=(shape[2] // TILE, tiles // part), in_...]
where the time goes in v2:
time: 421 us; the launch traced here: 419 us
  Pallas kernels  419 us (100%)
    pallas_call x1, Pallas kernels, on_device(): pl.pallas_call(functools.partial(fused_kernel, ra, rb), in_specs=[kept, w...  409 us
    pallas_call x1, Pallas kernels, unfold(): pl.pallas_call(unfold_kernel, grid=(shape[2] // TILE, tiles // part), in_...  10.8 us

profile of v2, /device:TPU:0, one launch (start us, length us, event | category | flops | bytes accessed | tf_op | source)
XLA Modules:
  0.0 419.4 jit_solution(12604438388852898858)
XLA Ops:
  0.0 408.7 %shard_map.64.in_ref = bf16[2,64,8,16,256]{4,3,2,1,0:T(8,128)(2,1)} custom-call(bf16[2,128,64,256]{3,2,1,0:T(8,128)(2,1)} %amp_ref.1, bf16[6,256,256]{2,1,0:T(8,128)(2,1)} %coupling_ref.1, s32[4,4,6]{2,1,0:T(4,128)} %bitcast.3, f32[6,64,128]{2,1,0:T(8,128)} %bitcast.2, bf16[2,512,512]{2,1,0:T(8,128)(2,1)} %first_ref.1, bf16[2,512,512]{2,1,0:T(8,128)(2,1)} %second_ref.1), custom_call_target="tpu_custom_call" | custom-call | tf_op jit(solution)/shard_map/pallas_call | solution.py:515
  408.7 10.8 %shard_map.65 = bf16[2,128,64,256]{3,2,1,0:T(8,128)(2,1)} custom-call(bf16[2,64,8,16,256]{4,3,2,1,0:T(8,128)(2,1)} %shard_map.64.in_ref), custom_call_target="tpu_custom_call" | custom-call | tf_op jit(solution)/shard_map/pallas_call | solution.py:485

commit v3 on v2

--- a/solution.py
+++ b/solution.py
@@ -88,9 +88,9 @@
     return out
 
 
-def fused_kernel(ra, rb, amp_ref, coupling_ref, pattern_ref, turned_ref, first_ref, second_ref, out_ref,
-                 lower, upper, left, right, turn, stage, first_mat, second_mat, weights_ref, radial_ref, near, far, lines,
-                 load_sem, store_sem, send_sem, recv_near, recv_far, recv_back, recv_home, rad_send, rad_recv):
+def fused_kernel(ra, rb, amp_ref, coupling_ref, pattern_ref, turned_ref, first_ref, second_ref, upper,
+                 lower, left, right, turn, stage, first_mat, second_mat, weights_ref, radial_ref, near, far, lines,
+                 load_sem, send_sem, recv_near, recv_far, recv_back, recv_home, rad_send, rad_recv):
     at_a, at_b = lax.axis_index("ra"), lax.axis_index("rb")
     bits_a, bits_b = ra.bit_length() - 1, rb.bit_length() - 1
     chunks = left.shape[1]
@@ -129,10 +129,6 @@
         slot = lax.rem(q, 2)
         return pltpu.make_async_copy(amp_ref.at[:, :, pl.ds(q * TILE, TILE)], stage.at[slot], load_sem.at[slot])
 
-    def store(q):
-        tile = pl.ds(q * TILE, TILE)
-        return pltpu.make_async_copy(upper.at[:, tile], out_ref.at[:, tile], store_sem)
-
     load(jnp.int32(0)).start()
     load(jnp.int32(1)).start()
 
@@ -309,7 +305,6 @@
 
     def finish_chunk(q):
         arrived(upper.at[:, pl.ds(q * TILE, TILE)], recv_home.at[q])
-        store(q).start()
 
     def near_all(q):
         for bp in range(pairs):
@@ -463,31 +458,44 @@
 
     lax.fori_loop(0, chunks + 1, closing, 0)
 
-    pltpu.make_async_copy(upper, out_ref, store_sem).wait()
     arrived(lower.at[:, 0:lower.shape[1] * (devices - 1) // devices], send_sem.at[2])
     arrived(right.at[:, :, :, :, 0:sixteens * (ra - 1) // ra], send_sem.at[3])
     arrived(far.at[0:rb - 1], rad_send)
 
 
-def unfold_kernel(in_ref, out_ref):
-    def group(g, carry):
-        for p in range(2):
-            turned = jnp.swapaxes(in_ref[p, :, g].astype(jnp.float32), 0, 1)
-            out_ref[p, pl.ds(g * TILE, TILE)] = turned.astype(jnp.bfloat16)
-        return carry
-
-    lax.fori_loop(0, in_ref.shape[2], group, 0)
+def unfold_kernel(in_ref, out_ref, stage, sem):
+    chunks = stage.shape[0]
+    tiles = stage.shape[2] // TILE
+    part = tiles // 2
+
+    def piece(n, carry):
+        q, first = lax.div(n, 2), lax.rem(n, 2) * part
+        for g in range(part):
+            for p in range(2):
+                rows = in_ref[p, pl.ds(q * TILE, TILE), first + g]
+                turned = jnp.swapaxes(rows.astype(jnp.float32), 0, 1)
+                stage[q, p, pl.ds((first + g) * TILE, TILE)] = turned.astype(jnp.bfloat16)
+        span = pl.ds(first * TILE, part * TILE)
+        pltpu.make_async_copy(
+            stage.at[q, :, span], out_ref.at[:, span, pl.ds(pl.multiple_of(q * TILE, TILE), TILE)], sem
+        ).start()
+        return carry
+
+    lax.fori_loop(0, 2 * chunks, piece, 0)
+    pltpu.make_async_copy(stage, stage, sem).wait()
 
 
 def unfold(folded, shape):
-    tiles = shape[1] // TILE
-    part = tiles // 2
     return pl.pallas_call(
         unfold_kernel,
-        grid=(shape[2] // TILE, tiles // part),
-        in_specs=[pl.BlockSpec((2, TILE, part, TILE, shape[3]), lambda q, g: (0, q, g, 0, 0))],
-        out_specs=pl.BlockSpec((2, part * TILE, TILE, shape[3]), lambda q, g: (0, g, q, 0)),
+        in_specs=[pl.BlockSpec(memory_space=pltpu.VMEM)],
+        out_specs=pl.BlockSpec(memory_space=pl.ANY),
         out_shape=jax.ShapeDtypeStruct(shape, jnp.bfloat16),
+        scratch_shapes=[
+            pltpu.VMEM((shape[2] // TILE, 2, shape[1], TILE, shape[3]), jnp.bfloat16),
+            pltpu.SemaphoreType.DMA(()),
+        ],
+        compiler_params=pltpu.CompilerParams(vmem_limit_bytes=24 * 2**20),
     )(folded)
 
 
@@ -515,10 +523,9 @@
     folded = pl.pallas_call(
         functools.partial(fused_kernel, ra, rb),
         in_specs=[kept, whole, pl.BlockSpec(memory_space=pltpu.SMEM), whole, whole, whole],
-        out_specs=kept,
-        out_shape=jax.ShapeDtypeStruct(flat, jnp.bfloat16),
+        out_specs=whole,
+        out_shape=pltpu.VMEM(flat, jnp.bfloat16),
         scratch_shapes=[
-            pltpu.VMEM(flat, jnp.bfloat16),
             pltpu.VMEM(flat, jnp.bfloat16),
             pltpu.VMEM(tall, jnp.bfloat16),
             pltpu.VMEM(tall, jnp.bfloat16),
@@ -531,11 +538,11 @@
             pltpu.VMEM((a_rows // HALF, b_rows, KTERMS * HALF), jnp.float32),
             pltpu.VMEM((rb, KTERMS, TILE, b_rows), jnp.float32),
             pltpu.VMEM((HALF, rb * KTERMS, b_rows), jnp.float32),
-            dma((2,)), dma(()), dma((4,)), dma((chunks * pairs,)), dma((2,)), dma((chunks * pairs,)), dma((chunks,)),
+            dma((2,)), dma((4,)), dma((chunks * pairs,)), dma((2,)), dma((chunks * pairs,)), dma((chunks,)),
             dma(()), dma(()),
         ],
         compiler_params=pltpu.CompilerParams(
-            collective_id=0, has_side_effects=True, vmem_limit_bytes=63 * 2**20
+            collective_id=0, has_side_effects=True, vmem_limit_bytes=55 * 2**20
         ),
     )(amplitude, coupling, pattern.transpose(1, 2, 0), radial.transpose(0, 2, 1), first_prop, second_prop)
     return unfold(folded, amplitude.shape)

time: 421 us -> 413 us (0.981)
  Pallas kernels: 419 us -> 413 us
    pallas_call x1, Pallas kernels: 10.8 us -> 4.84 us  [unfold(): pl.pallas_call(unfold_kernel, in_specs=[pl.BlockSpec(memory_space=pltpu.V...]
where the time goes in v3:
time: 413 us
  Pallas kernels  413 us (100%)
    pallas_call x1, Pallas kernels, on_device(): pl.pallas_call(functools.partial(fused_kernel, ra, rb), in_specs=[kept, w...  408 us

profile of v3, /device:TPU:0, one launch (start us, length us, event | category | flops | bytes accessed | tf_op | source)
XLA Modules:
  0.0 412.7 jit_solution(4933098317761977338)
XLA Ops:
  0.0 407.8 %shard_map.64.in_ref = bf16[2,64,8,16,256]{4,3,2,1,0:T(8,128)(2,1)S(1)} custom-call(bf16[2,128,64,256]{3,2,1,0:T(8,128)(2,1)} %amp_ref.1, bf16[6,256,256]{2,1,0:T(8,128)(2,1)} %coupling_ref.1, s32[4,4,6]{2,1,0:T(4,128)} %bitcast.3, f32[6,64,128]{2,1,0:T(8,128)} %bitcast.2, bf16[2,512,512]{2,1,0:T(8,128)(2,1)} %first_ref.1, bf16[2,512,512]{2,1,0:T(8,128)(2,1)} %second_ref.1), custom_call_target="tpu_custom_call" | custom-call | tf_op jit(solution)/shard_map/pallas_call | solution.py:523
  407.8 4.8 %shard_map.65 = bf16[2,128,64,256]{3,2,1,0:T(8,128)(2,1)} custom-call(bf16[2,64,8,16,256]{4,3,2,1,0:T(8,128)(2,1)S(1)} %shard_map.64.in_ref), custom_call_target="tpu_custom_call" | custom-call | tf_op jit(solution)/shard_map/pallas_call | solution.py:489

commit v4 on v3

--- a/solution.py
+++ b/solution.py
@@ -76,7 +76,6 @@
     return amplitude
 
 
-BACK_LEAD = 2
 FAR_LEAD = 2
 
 
@@ -119,11 +118,22 @@
     barrier = pltpu.get_barrier_semaphore()
 
     def greet(d, carry):
-        to_a, to_b = partner(d)
+        to_a, to_b = partner(devices - d)
         pl.semaphore_signal(barrier, inc=1, device_id=(to_a, to_b), device_id_type=MESH)
         return carry
 
     lax.fori_loop(1, devices, greet, 0)
+
+    every_lane = pl.ds(0, channels)
+    sheets = channels // LANES
+    sheet = [pl.ds(s * LANES, LANES) for s in range(sheets)]
+    last = chunks * pairs
+
+    def edge(c):
+        return (c == 0) | (c == last - 1)
+
+    def spare(c, s):
+        return last + lax.div(c, last - 1) * sheets + s
 
     def load(q):
         slot = lax.rem(q, 2)
@@ -167,9 +177,10 @@
                 total[p] = term if k == 0 else total[p] + term
         return planes[0].astype(jnp.float32) + total[1], planes[1].astype(jnp.float32) - total[0]
 
-    def kick_chunk(q):
+    def kick_chunk(q, first=0, stop=None):
         slot = lax.rem(q, 2)
-        load(q).wait()
+        if first == 0:
+            load(q).wait()
 
         def group(g, carry):
             count = TILE * TILE
@@ -188,17 +199,18 @@
                 lower[p, pl.ds(q * TILE, TILE), g] = turned
             return carry
 
-        lax.fori_loop(0, a_tiles, group, 0)
-
-        @pl.when(q + 2 < chunks)
-        def _():
-            load(q + 2).start()
-
-    def near_start(q, bp, d):
-        to = flip(at_a, d, bits_a)
-        source = lower.at[:, pl.ds(q * TILE + to * per + bp * 2, 2)]
-        target = left.at[:, q, bp, :, pl.ds(at_a * a_tiles, a_tiles)]
-        sem = recv_near.at[q * pairs + bp]
+        lax.fori_loop(first, a_tiles if stop is None else stop, group, 0)
+        if stop is None:
+            @pl.when(q + 2 < chunks)
+            def _():
+                load(q + 2).start()
+
+    def near_start(q, bp, d, first=0, count=None, lanes=every_lane, sem=None):
+        to = flip(at_a, d, bits_a) if d < ra // 2 else opposite + d - ra // 2
+        count = a_tiles if count is None else count
+        source = lower.at[:, pl.ds(q * TILE + to * per + bp * 2, 2), pl.ds(first, count), :, lanes]
+        target = left.at[:, q, bp, :, pl.ds(at_a * a_tiles + first, count), :, lanes]
+        sem = recv_near.at[q * pairs + bp if sem is None else sem]
         if d == 0:
             pltpu.make_async_copy(source, target, sem).start()
         else:
@@ -207,10 +219,10 @@
                 device_id=(to, at_b), device_id_type=MESH,
             ).start()
 
-    def home_start(q, bp, d):
+    def home_start(q, bp, d, lanes=every_lane):
         to = flip(at_a, d, bits_a)
-        source = right.at[:, q, bp, :, pl.ds(to * a_tiles, a_tiles)]
-        target = upper.at[:, pl.ds(q * TILE + at_a * per + bp * 2, 2)]
+        source = right.at[:, q, bp, :, pl.ds(to * a_tiles, a_tiles), :, lanes]
+        target = upper.at[:, pl.ds(q * TILE + at_a * per + bp * 2, 2), :, :, lanes]
         if d == 0:
             pltpu.make_async_copy(source, target, recv_home.at[q]).start()
         else:
@@ -219,6 +231,7 @@
                 device_id=(to, at_b), device_id_type=MESH,
             ).start()
 
+    opposite = (1 - lax.div(at_a, ra // 2)) * (ra // 2)
     near_order = list(range(ra // 2, ra)) + list(range(1, ra // 2)) + [0]
     side = devices // 2
 
@@ -226,16 +239,16 @@
         index = (i * rb + j) * 2 + h
         return lax.div(index, sixteens), lax.rem(index, sixteens)
 
-    def far_start(c, h, crossing):
+    def far_start(c, h, crossing, lanes=every_lane):
         q, bp = lax.div(c, pairs), lax.rem(c, pairs)
         row = h * halfway + at_b * chunks + q
-        target = upper.at[:, row, at_a * pairs + bp]
+        target = upper.at[:, row, at_a * pairs + bp, :, lanes]
 
         def one(d, carry):
             to_a, to_b = partner(d)
             high, low = place(to_a, to_b, h)
             pltpu.make_async_remote_copy(
-                src_ref=right.at[:, q, bp, high, low], dst_ref=target,
+                src_ref=right.at[:, q, bp, high, low, :, lanes], dst_ref=target,
                 send_sem=send_sem.at[1], recv_sem=recv_far.at[h], device_id=(to_a, to_b), device_id_type=MESH,
             ).start()
             return carry
@@ -245,18 +258,19 @@
         else:
             lax.fori_loop(1, side, one, 0)
             high, low = place(at_a, at_b, h)
-            pltpu.make_async_copy(right.at[:, q, bp, high, low], target, recv_far.at[h]).start()
-
-    def back_start(c, h, crossing):
+            pltpu.make_async_copy(right.at[:, q, bp, high, low, :, lanes], target, recv_far.at[h]).start()
+
+    def back_start(c, h, crossing, lanes=every_lane, sem=None):
         q, bp = lax.div(c, pairs), lax.rem(c, pairs)
         high, low = place(at_a, at_b, h)
-        target = left.at[:, q, bp, high, low]
+        target = left.at[:, q, bp, high, low, :, lanes]
+        sem = recv_back.at[c if sem is None else sem]
 
         def one(d, carry):
             to_a, to_b = partner(d)
             pltpu.make_async_remote_copy(
-                src_ref=lower.at[:, h * halfway + to_b * chunks + q, to_a * pairs + bp], dst_ref=target,
-                send_sem=send_sem.at[2], recv_sem=recv_back.at[c], device_id=(to_a, to_b), device_id_type=MESH,
+                src_ref=lower.at[:, h * halfway + to_b * chunks + q, to_a * pairs + bp, :, lanes], dst_ref=target,
+                send_sem=send_sem.at[2], recv_sem=sem, device_id=(to_a, to_b), device_id_type=MESH,
             ).start()
             return carry
 
@@ -265,7 +279,7 @@
         else:
             lax.fori_loop(1, side, one, 0)
             pltpu.make_async_copy(
-                lower.at[:, h * halfway + at_b * chunks + q, at_a * pairs + bp], target, recv_back.at[c]
+                lower.at[:, h * halfway + at_b * chunks + q, at_a * pairs + bp, :, lanes], target, sem
             ).start()
 
     def every(action):
@@ -278,42 +292,82 @@
     def arrived(ref, sem):
         pltpu.make_async_copy(ref, ref, sem).wait()
 
-    def first_chunk(c):
+    def first_chunk(c, lanes=every_lane, sem=None):
         q, bp = lax.div(c, pairs), lax.rem(c, pairs)
-        arrived(left.at[:, q, bp], recv_near.at[c])
+        arrived(left.at[:, q, bp, :, :, :, lanes], recv_near.at[c if sem is None else sem])
         made = []
         for par in range(2):
-            both = jnp.concatenate([left[p, q, bp, par].reshape(depth, channels) for p in range(2)], axis=0)
+            both = jnp.concatenate([
+                left[p, q, bp, par, :, :, lanes].reshape(depth, lanes.size) for p in range(2)
+            ], axis=0)
             made.append(jnp.dot(first_mat[...], both, preferred_element_type=jnp.float32))
         for p in range(2):
-            parts = [m[p * depth:(p + 1) * depth].reshape(groups, HALF, channels) for m in made]
+            parts = [m[p * depth:(p + 1) * depth].reshape(groups, HALF, lanes.size) for m in made]
             mixed = jnp.concatenate(parts, axis=1).astype(jnp.bfloat16)
-            right[p, q, bp] = mixed.reshape(2, sixteens, TILE, channels)
-
-    def last_chunk(c):
+            right[p, q, bp, :, :, :, lanes] = mixed.reshape(2, sixteens, TILE, lanes.size)
+        far_start(c, 0, False, lanes)
+        far_start(c, 1, False, lanes)
+
+    def last_chunk(c, lanes=every_lane):
         q, bp = lax.div(c, pairs), lax.rem(c, pairs)
-        arrived(left.at[:, q, bp], recv_back.at[c])
-        wide = [left[p, q, bp].reshape(groups, TILE, channels).astype(jnp.float32) for p in range(2)]
+        wide = [
+            left[p, q, bp, :, :, :, lanes].reshape(groups, TILE, lanes.size).astype(jnp.float32) for p in range(2)
+        ]
         for par in range(2):
             both = jnp.concatenate([
-                w[:, par * HALF:(par + 1) * HALF].reshape(depth, channels).astype(jnp.bfloat16) for w in wide
+                w[:, par * HALF:(par + 1) * HALF].reshape(depth, lanes.size).astype(jnp.bfloat16) for w in wide
             ], axis=0)
             made = jnp.dot(first_mat[...], both, preferred_element_type=jnp.float32)
             for p in range(2):
-                part = made[p * depth:(p + 1) * depth].reshape(sixteens, TILE, channels)
-                right[p, q, bp, par] = part.astype(jnp.bfloat16)
+                part = made[p * depth:(p + 1) * depth].reshape(sixteens, TILE, lanes.size)
+                right[p, q, bp, par, :, :, lanes] = part.astype(jnp.bfloat16)
+        for d in near_order:
+            home_start(q, bp, d, lanes)
 
     def finish_chunk(q):
         arrived(upper.at[:, pl.ds(q * TILE, TILE)], recv_home.at[q])
 
+        @pl.when(q < chunks - 1)
+        def _():
+            def group(g, carry):
+                for p in range(2):
+                    rows = upper[p, pl.ds(q * TILE, TILE), g].astype(jnp.float32)
+                    upper[p, pl.ds(q * TILE, TILE), g] = jnp.swapaxes(rows, 0, 1).astype(jnp.bfloat16)
+                return carry
+
+            lax.fori_loop(0, a_tiles, group, 0)
+
     def near_all(q):
-        for bp in range(pairs):
+        for bp in range(pairs - 1):
             for d in near_order:
                 near_start(q, bp, d)
 
-    kick_chunk(jnp.int32(0))
+        @pl.when(q < chunks - 1)
+        def _():
+            for d in near_order:
+                near_start(q, pairs - 1, d)
+
+        @pl.when(q == chunks - 1)
+        def _():
+            for s in range(sheets):
+                for d in near_order:
+                    near_start(q, pairs - 1, d, lanes=sheet[s], sem=spare(last - 1, s))
+
+    start = jnp.int32(0)
+    early = a_tiles // 2
+    kick_chunk(start, 0, early)
     pl.semaphore_wait(barrier, devices - 1)
-    near_all(jnp.int32(0))
+    for d in near_order:
+        near_start(start, 0, d, 0, early, sheet[0], spare(start, 0))
+    kick_chunk(start, early)
+    for d in near_order:
+        near_start(start, 0, d, early, early, sheet[0], spare(start, 0))
+    for s in range(1, sheets):
+        for d in near_order:
+            near_start(start, 0, d, lanes=sheet[s], sem=spare(start, s))
+    for bp in range(1, pairs):
+        for d in near_order:
+            near_start(start, bp, d)
 
     def rad_copy(n):
         to = flip(at_b, n, bits_b)
@@ -345,9 +399,15 @@
             near_all(t)
 
         def one(c, carry):
-            first_chunk(c)
-            far_start(c, 0, False)
-            far_start(c, 1, False)
+            @pl.when(edge(c))
+            def _():
+                for s in range(sheets):
+                    first_chunk(c, sheet[s], spare(c, s))
+
+            @pl.when(jnp.logical_not(edge(c)))
+            def _():
+                first_chunk(c)
+
             return carry
 
         lax.fori_loop((t - 1) * pairs, t * pairs, one, 0)
@@ -364,8 +424,7 @@
     arrived(lower.at[:, 0:lower.shape[1] * (ra - 1) // ra], send_sem.at[0])
     arrived(far, rad_recv)
 
-    width = LANES * 1
-    sheets = channels // width
+    width = LANES
     block = a_tiles * TILE
 
     def middle(h, carry):
@@ -426,25 +485,50 @@
 
     lax.fori_loop(0, 2, middle, 0)
 
-    def rest(c, carry):
-        back_start(c, 0, False)
-        back_start(c, 1, False)
-        return carry
-
-    lax.fori_loop(0, BACK_LEAD, rest, 0)
+    def part(c, s):
+        @pl.when(edge(c))
+        def _():
+            for h in range(2):
+                back_start(c, h, False, sheet[s], spare(c, s))
+
+        @pl.when(jnp.logical_not(edge(c)))
+        def _():
+            back_start(c, s, False)
+
+    part(jnp.int32(0), 0)
+    part(jnp.int32(0), 1)
+    part(jnp.int32(1), 0)
     arrived(right.at[:, :, :, :, 0:sixteens * (devices - 1) // devices], send_sem.at[1])
 
     def closing(t, carry):
         @pl.when(t < chunks)
         def _():
             def one(c, carry):
-                last_chunk(c)
-                for d in near_order:
-                    home_start(t, lax.rem(c, pairs), d)
-
-                @pl.when(c + BACK_LEAD < chunks * pairs)
+                bp = lax.rem(c, pairs)
+
+                def onward():
+                    @pl.when(c + 1 < last)
+                    def _():
+                        part(c + 1, 1)
+
+                    @pl.when(c + 2 < last)
+                    def _():
+                        part(c + 2, 0)
+
+                @pl.when(jnp.logical_not(edge(c)))
                 def _():
-                    rest(c + BACK_LEAD, 0)
+                    arrived(left.at[:, t, bp], recv_back.at[c])
+                    onward()
+                    last_chunk(c)
+
+                @pl.when(edge(c))
+                def _():
+                    arrived(left.at[:, t, bp, 0], recv_back.at[c])
+                    for s in range(sheets):
+                        arrived(left.at[:, t, bp, 0, :, :, sheet[s]], recv_back.at[spare(c, s)])
+                        if s == sheets - 1:
+                            onward()
+                        last_chunk(c, sheet[s])
 
                 return carry
 
@@ -464,25 +548,28 @@
 
 
 def unfold_kernel(in_ref, out_ref, stage, sem):
-    chunks = stage.shape[0]
-    tiles = stage.shape[2] // TILE
-    part = tiles // 2
-
-    def piece(n, carry):
-        q, first = lax.div(n, 2), lax.rem(n, 2) * part
-        for g in range(part):
-            for p in range(2):
-                rows = in_ref[p, pl.ds(q * TILE, TILE), first + g]
-                turned = jnp.swapaxes(rows.astype(jnp.float32), 0, 1)
-                stage[q, p, pl.ds((first + g) * TILE, TILE)] = turned.astype(jnp.bfloat16)
-        span = pl.ds(first * TILE, part * TILE)
-        pltpu.make_async_copy(
-            stage.at[q, :, span], out_ref.at[:, span, pl.ds(pl.multiple_of(q * TILE, TILE), TILE)], sem
-        ).start()
-        return carry
-
-    lax.fori_loop(0, 2 * chunks, piece, 0)
-    pltpu.make_async_copy(stage, stage, sem).wait()
+    tiles = stage.shape[1] // TILE
+    done = in_ref.shape[1] // TILE - 1
+
+    def ready(n, carry):
+        q, g = lax.div(n, tiles), lax.rem(n, tiles)
+        at = pl.ds(pl.multiple_of(q * TILE, TILE), TILE)
+        pltpu.make_async_copy(in_ref.at[:, at, g], out_ref.at[:, pl.ds(g * TILE, TILE), at], sem).start()
+        return carry
+
+    lax.fori_loop(0, done * tiles, ready, 0)
+    at = pl.ds(done * TILE, TILE)
+
+    def group(g, carry):
+        span = pl.ds(g * TILE, TILE)
+        for p in range(2):
+            turned = jnp.swapaxes(in_ref[p, at, g].astype(jnp.float32), 0, 1)
+            stage[p, span] = turned.astype(jnp.bfloat16)
+        pltpu.make_async_copy(stage.at[:, span], out_ref.at[:, span, at], sem).start()
+        return carry
+
+    lax.fori_loop(0, tiles, group, 0)
+    pltpu.make_async_copy(in_ref, in_ref, sem).wait()
 
 
 def unfold(folded, shape):
@@ -492,10 +579,10 @@
         out_specs=pl.BlockSpec(memory_space=pl.ANY),
         out_shape=jax.ShapeDtypeStruct(shape, jnp.bfloat16),
         scratch_shapes=[
-            pltpu.VMEM((shape[2] // TILE, 2, shape[1], TILE, shape[3]), jnp.bfloat16),
+            pltpu.VMEM((2, shape[1], TILE, shape[3]), jnp.bfloat16),
             pltpu.SemaphoreType.DMA(()),
         ],
-        compiler_params=pltpu.CompilerParams(vmem_limit_bytes=24 * 2**20),
+        compiler_params=pltpu.CompilerParams(vmem_limit_bytes=16 * 2**20),
     )(folded)
 
 
@@ -538,7 +625,8 @@
             pltpu.VMEM((a_rows // HALF, b_rows, KTERMS * HALF), jnp.float32),
             pltpu.VMEM((rb, KTERMS, TILE, b_rows), jnp.float32),
             pltpu.VMEM((HALF, rb * KTERMS, b_rows), jnp.float32),
-            dma((2,)), dma((4,)), dma((chunks * pairs,)), dma((2,)), dma((chunks * pairs,)), dma((chunks,)),
+            dma((2,)), dma((4,)), dma((chunks * pairs + 2 * channels // LANES,)), dma((2,)),
+            dma((chunks * pairs + 2 * channels // LANES,)), dma((chunks,)),
             dma(()), dma(()),
         ],
         compiler_params=pltpu.CompilerParams(

time: 413 us -> 406 us (0.983)
  Pallas kernels: 413 us -> 406 us
    pallas_call x1, Pallas kernels: 408 us -> 403 us  [on_device(): pl.pallas_call(functools.partial(fused_kernel, ra, rb), in_specs=[kept, w...]
where the time goes in v4:
time: 406 us
  Pallas kernels  406 us (100%)
    pallas_call x1, Pallas kernels, on_device(): pl.pallas_call(functools.partial(fused_kernel, ra, rb), in_specs=[kept, w...  403 us

profile of v4, /device:TPU:0, one launch (start us, length us, event | category | flops | bytes accessed | tf_op | source)
XLA Modules:
  0.0 406.3 jit_solution(1429682258620151515)
XLA Ops:
  0.0 402.8 %shard_map.64.in_ref = bf16[2,64,8,16,256]{4,3,2,1,0:T(8,128)(2,1)S(1)} custom-call(bf16[2,128,64,256]{3,2,1,0:T(8,128)(2,1)} %amp_ref.1, bf16[6,256,256]{2,1,0:T(8,128)(2,1)} %coupling_ref.1, s32[4,4,6]{2,1,0:T(4,128)} %bitcast.3, f32[6,64,128]{2,1,0:T(8,128)} %bitcast.2, bf16[2,512,512]{2,1,0:T(8,128)(2,1)} %first_ref.1, bf16[2,512,512]{2,1,0:T(8,128)(2,1)} %second_ref.1), custom_call_target="tpu_custom_call" | custom-call | tf_op jit(solution)/shard_map/pallas_call | solution.py:610
  402.8 3.3 shard_map.65

commit v5 on v4

--- a/solution.py
+++ b/solution.py
@@ -76,7 +76,7 @@
     return amplitude
 
 
-FAR_LEAD = 2
+FAR_LEAD = 3
 
 
 def flip(value, mask, bits):
@@ -156,12 +156,13 @@
             masked.append(coupling_ref[k, i * size_block:(i + 1) * size_block].astype(jnp.float32) * keep)
         weights_ref[k] = jnp.transpose(jnp.concatenate(masked, axis=0)).astype(jnp.bfloat16)
 
-    for k in range(KTERMS):
-        radial_ref[k] = jnp.transpose(turned_ref[k])
+    duos = KTERMS // 2
+    for m in range(duos):
+        radial_ref[m] = jnp.transpose(turned_ref[2 * m:2 * m + 2].reshape(2 * b_rows, radial_ref.shape[1]))
 
     def lay(g, carry):
         at = pl.ds(pl.multiple_of(g * HALF, HALF), HALF)
-        near[g] = jnp.transpose(radial_ref[:, at].reshape(KTERMS * HALF, b_rows))
+        near[g] = jnp.transpose(radial_ref[:, at].reshape(duos * HALF, 2 * b_rows))
         return carry
 
     lax.fori_loop(0, radial_ref.shape[1] // HALF, lay, 0)
@@ -185,12 +186,16 @@
         def group(g, carry):
             count = TILE * TILE
             planes = [stage[slot, p, pl.ds(g * TILE, TILE)].reshape(count, channels) for p in range(2)]
-            laid = [near[g * 2 + n, pl.ds(pl.multiple_of(q * TILE, TILE), TILE)] for n in range(2)]
+            laid = [[
+                near[g * 2 + n, pl.ds(pl.multiple_of(odd * b_rows + q * TILE, TILE), TILE)] for n in range(2)
+            ] for odd in range(2)]
 
             def factor_of(k):
+                m, odd = divmod(k, 2)
                 return jnp.concatenate([
-                    jnp.broadcast_to(laid[n // HALF][:, k * HALF + n % HALF:k * HALF + n % HALF + 1], (TILE, channels))
-                    for n in range(TILE)
+                    jnp.broadcast_to(
+                        laid[odd][n // HALF][:, m * HALF + n % HALF:m * HALF + n % HALF + 1], (TILE, channels)
+                    ) for n in range(TILE)
                 ], axis=0)
 
             result = kick(planes, factor_of, count)
@@ -434,7 +439,7 @@
         def _():
             lax.fori_loop(FAR_LEAD, chunks * pairs, crossing, 1)
 
-        pieces = far[:, :, pl.ds(pl.multiple_of(h * HALF, HALF), HALF)].reshape(rb * KTERMS, HALF, b_rows)
+        pieces = far[:, :, pl.ds(pl.multiple_of(h * HALF, HALF), HALF)].reshape(rb * duos, HALF, 2 * b_rows)
         lines[...] = jnp.swapaxes(pieces, 0, 1)
 
         def spread(m, carry):
@@ -456,8 +461,10 @@
             laid = jnp.transpose(lines[a])
 
             def factor_of(k):
+                m, odd = divmod(k, 2)
+                half = laid[odd * b_rows:(odd + 1) * b_rows]
                 return jnp.concatenate([
-                    jnp.broadcast_to(laid[:, n * KTERMS + k:n * KTERMS + k + 1], (b_rows, channels)) for n in range(rb)
+                    jnp.broadcast_to(half[:, n * duos + m:n * duos + m + 1], (b_rows, channels)) for n in range(rb)
                 ], axis=0)
 
             kicked = kick([made[:size], made[size:]], factor_of, size)
@@ -595,7 +602,7 @@
     fits = (
         channels == 2 * LANES and ra & (ra - 1) == 0 and rb == HALF and ra in (2, 4) and n_a == n_b
         and n_a == TILE * devices and n_b == TILE * devices and a_rows % TILE == 0 and b_rows % TILE == 0
-        and chunks % 2 == 0 and chunks == ra and a_rows == TILE * HALF and b_rows <= LANES
+        and chunks % 2 == 0 and chunks == ra and a_rows == TILE * HALF and 2 * b_rows == LANES and KTERMS % 2 == 0
     )
     if not fits:
         return plain(amplitude, coupling, pattern, radial, first_prop, second_prop)
@@ -621,10 +628,10 @@
             pltpu.VMEM((2 * n_a, 2 * n_a), jnp.bfloat16),
             pltpu.VMEM((2 * n_b, 2 * n_b), jnp.bfloat16),
             pltpu.VMEM((KTERMS, channels, channels), jnp.bfloat16),
-            pltpu.VMEM((KTERMS, a_rows, b_rows), jnp.float32),
-            pltpu.VMEM((a_rows // HALF, b_rows, KTERMS * HALF), jnp.float32),
-            pltpu.VMEM((rb, KTERMS, TILE, b_rows), jnp.float32),
-            pltpu.VMEM((HALF, rb * KTERMS, b_rows), jnp.float32),
+            pltpu.VMEM((KTERMS // 2, a_rows, 2 * b_rows), jnp.float32),
+            pltpu.VMEM((a_rows // HALF, 2 * b_rows, KTERMS // 2 * HALF), jnp.float32),
+            pltpu.VMEM((rb, KTERMS // 2, TILE, 2 * b_rows), jnp.float32),
+            pltpu.VMEM((HALF, rb * KTERMS // 2, 2 * b_rows), jnp.float32),
             dma((2,)), dma((4,)), dma((chunks * pairs + 2 * channels // LANES,)), dma((2,)),
             dma((chunks * pairs + 2 * channels // LANES,)), dma((chunks,)),
             dma(()), dma(()),

time: 406 us -> 403 us (level)
  no operation moved by 1% of the time
where the time goes in v5:
time: 403 us; the launch traced here: 402 us
  Pallas kernels  402 us (100%)
    pallas_call x1, Pallas kernels, on_device(): pl.pallas_call(functools.partial(fused_kernel, ra, rb), in_specs=[kept, w...  399 us

profile of v5, /device:TPU:0, one launch (start us, length us, event | category | flops | bytes accessed | tf_op | source)
XLA Modules:
  0.0 402.5 jit_solution(2744231533319870019)
XLA Ops:
  0.0 399.0 %shard_map.64.in_ref = bf16[2,64,8,16,256]{4,3,2,1,0:T(8,128)(2,1)S(1)} custom-call(bf16[2,128,64,256]{3,2,1,0:T(8,128)(2,1)} %amp_ref.1, bf16[6,256,256]{2,1,0:T(8,128)(2,1)} %coupling_ref.1, s32[4,4,6]{2,1,0:T(4,128)} %bitcast.3, f32[6,64,128]{2,1,0:T(8,128)} %bitcast.2, bf16[2,512,512]{2,1,0:T(8,128)(2,1)} %first_ref.1, bf16[2,512,512]{2,1,0:T(8,128)(2,1)} %second_ref.1), custom_call_target="tpu_custom_call" | custom-call | tf_op jit(solution)/shard_map/pallas_call | solution.py:617
  399.0 3.3 shard_map.65

commit v6 on v5

--- a/solution.py
+++ b/solution.py
@@ -359,14 +359,14 @@
                     near_start(q, pairs - 1, d, lanes=sheet[s], sem=spare(last - 1, s))
 
     start = jnp.int32(0)
-    early = a_tiles // 2
+    early = a_tiles * 3 // 4
     kick_chunk(start, 0, early)
     pl.semaphore_wait(barrier, devices - 1)
     for d in near_order:
         near_start(start, 0, d, 0, early, sheet[0], spare(start, 0))
     kick_chunk(start, early)
     for d in near_order:
-        near_start(start, 0, d, early, early, sheet[0], spare(start, 0))
+        near_start(start, 0, d, early, a_tiles - early, sheet[0], spare(start, 0))
     for s in range(1, sheets):
         for d in near_order:
             near_start(start, 0, d, lanes=sheet[s], sem=spare(start, s))

time: 403 us -> 404 us (level)
  no operation moved by 1% of the time
where the time goes in v6:
time: 404 us
  Pallas kernels  404 us (100%)
    pallas_call x1, Pallas kernels, on_device(): pl.pallas_call(functools.partial(fused_kernel, ra, rb), in_specs=[kept, w...  401 us

profile of v6, /device:TPU:0, one launch (start us, length us, event | category | flops | bytes accessed | tf_op | source)
XLA Modules:
  0.0 404.2 jit_solution(147100033420215506)
XLA Ops:
  0.0 400.8 %shard_map.64.in_ref = bf16[2,64,8,16,256]{4,3,2,1,0:T(8,128)(2,1)S(1)} custom-call(bf16[2,128,64,256]{3,2,1,0:T(8,128)(2,1)} %amp_ref.1, bf16[6,256,256]{2,1,0:T(8,128)(2,1)} %coupling_ref.1, s32[4,4,6]{2,1,0:T(4,128)} %bitcast.3, f32[6,64,128]{2,1,0:T(8,128)} %bitcast.2, bf16[2,512,512]{2,1,0:T(8,128)(2,1)} %first_ref.1, bf16[2,512,512]{2,1,0:T(8,128)(2,1)} %second_ref.1), custom_call_target="tpu_custom_call" | custom-call | tf_op jit(solution)/shard_map/pallas_call | solution.py:617
  400.8 3.3 shard_map.65
